TPU v7x, 128 devices: a whole 4x4x4 slice. The times are simulated.
128 devices in a mesh: frag: 4 (over y_hi, core), aux: 16 (over z, x), orb: 2 (over y_lo).
Axes of the slice: x: 4, y: 4 (y_hi: 2, y_lo: 2; y = y_hi * 2 + y_lo), z: 4, core: 2. Of those that a mesh axis runs over, the one named last changes fastest.
Arguments:
- density: bfloat16 [16384, 2, 8192], P('frag', 'orb', 'aux'), may hold values from -0.046875 to 0.046875
- bath: bfloat16 [16, 2, 8192, 128], P('frag', 'orb', 'aux'), may hold values from -1 to 1
- factor: bfloat16 [16384, 16384], P('orb', 'aux'), may hold values from -6 to 6
- frag_index: int32 [16, 128], replicated, may hold values from 0 to 16383, as said below
- nfrag: int32 [16], replicated, may hold values from 1 to 128
- nbath: int32 [16], replicated, may hold values from 1 to 128
Outputs:
- projected: bfloat16 [16, 256, 16384], P('frag', 'orb', 'aux')
Inputs may be any that keep to these rules, and one draw needn't show every extreme that they name: `frag_index`: the 128 entries of one fragment's row are distinct basis functions; entries at or past nfrag are not read.
All inputs are finite; a program needn't handle non-finite values.
Results may differ from a plain program's by a relative error of at most 0.0049.
Values may be sent and summed in bfloat16 or wider, within the bound.
A program may use at most 128 MiB of HBM per device.

v0:
```python
import jax
import jax.numpy as jnp
from jax import lax
from jax.sharding import PartitionSpec as P


def per_device(density, bath, factor, frag_index, nfrag, nbath):
    local_rows = density.shape[0]
    block_cols = density.shape[2]
    density_local = density.reshape(local_rows, block_cols)
    group_size = bath.shape[0]
    frag_max = frag_index.shape[1]
    bath_max = bath.shape[3]
    frag_count = frag_index.shape[0]
    row_offset = lax.axis_index("frag") * local_rows
    local_index = frag_index - row_offset
    owned_rows = (local_index >= 0) & (local_index < local_rows)
    picked = jnp.take(density_local, jnp.clip(local_index, 0, local_rows - 1).reshape(-1), axis=0)
    picked = picked.reshape(frag_count, frag_max, block_cols)
    picked = jnp.where(owned_rows[:, :, None], picked, jnp.zeros_like(picked))
    gathered_rows = (
        lax.psum_scatter(picked, "frag", scatter_dimension=0, tiled=True)
        .astype(jnp.float32)
        .astype(jnp.bfloat16)
    )
    first_frag = lax.axis_index("frag") * group_size
    my_nfrag = lax.dynamic_slice_in_dim(nfrag, first_frag, group_size)
    my_nbath = lax.dynamic_slice_in_dim(nbath, first_frag, group_size)
    frag_live = jnp.arange(frag_max, dtype=jnp.int32)[None, :] < my_nfrag[:, None]
    bath_live = jnp.arange(bath_max, dtype=jnp.int32)[None, :] < my_nbath[:, None]
    gathered_rows = jnp.where(frag_live[:, :, None], gathered_rows, jnp.zeros_like(gathered_rows))
    bath_cols = bath.reshape(group_size, block_cols, bath_max)
    bath_cols = jnp.where(bath_live[:, None, :], bath_cols, jnp.zeros_like(bath_cols))
    initial = jnp.concatenate([jnp.swapaxes(gathered_rows, 1, 2), bath_cols], axis=2)
    live_cols = jnp.concatenate([frag_live, bath_live], axis=1).astype(jnp.float32)
    kmax_cols = initial.shape[2]
    identity_pad = jnp.eye(kmax_cols, dtype=jnp.float32)[None] * (1.0 - live_cols)[:, :, None]
    gram_part = jnp.einsum("fmk,fml->fkl", initial, initial, preferred_element_type=jnp.float32)
    gram_total = lax.psum(gram_part, ("aux", "orb")) + identity_pad
    cholesky_low = jnp.linalg.cholesky(gram_total)
    coeffs = lax.linalg.triangular_solve(
        cholesky_low, initial.astype(jnp.float32), left_side=False, lower=True, transpose_a=True
    )
    coeffs = coeffs.astype(jnp.bfloat16)
    partial_value = jnp.einsum(
        "fmk,mq->fkq",
        lax.all_gather(coeffs, "aux", axis=1, tiled=True),
        factor,
        preferred_element_type=jnp.float32,
    )
    summed = lax.psum_scatter(partial_value, "orb", scatter_dimension=1, tiled=True)
    return summed.astype(jnp.bfloat16)


def solution(mesh):
    placed = (
        P("frag", "orb", "aux"),
        P("frag", "orb", "aux", None),
        P("orb", "aux"),
        P(),
        P(),
        P(),
    )
    return jax.shard_map(
        per_device, mesh=mesh, in_specs=placed, out_specs=P("frag", "orb", "aux"), check_vma=False
    )
```

profile of v0, /device:TPU:1, one launch (start us, length us, event | category | flops | bytes accessed | tf_op | source)
XLA Modules:
  0.0 812.8 jit_solution(12678690382864565310)
XLA Ops:
  6.5 0.7 compare_and_fusion
  7.3 10.3 %gather_fusion = bf16[2048,512]{1,0:T(8,128)(2,1)S(1)} fusion(bf16[4096,512]{1,0:T(8,128)(2,1)} %bitcast.50, s32[2048]{0:T(1024)S(1)} %broadcast_clamp_fusion), kind=kCustom, calls=%fused_computation | custom fusion | bytes 4202496 | tf_op jit(solution)/shard_map/jit(_take)/gather | solution.py:18
  17.6 2.4 copy.24
  20.0 3.2 select_select_fusion
  23.3 0.6 copy-done.5
  24.3 40.2 %reduce-scatter.3.cloned.1.call-done = bf16[4,128,512]{1,2,0:T(8,128)(2,1)} async-done(((bf16[16,128,512]{1,2,0:T(8,128)(2,1)}), bf16[4,128,512]{1,2,0:T(8,128)(2,1)}) %reduce-scatter.3.cloned.1.call-update) | async-done | bytes 524304 | tf_op jit(solution)/shard_map/reduce_scatter | solution.py:22
  64.5 1.1 fusion.8
  65.6 1.5 fusion.2
  67.1 0.2 all-gather.2.cloned.1.call-start
  67.5 286.9 %all-reduce.3.cloned.1.call-done = f32[4,256,256]{1,2,0:T(8,128)} async-done(((f32[4,256,256]{1,2,0:T(8,128)}), f32[4,256,256]{1,2,0:T(8,128)}) %all-reduce.3.cloned.1.call-update) | async-done | bytes 1048592 | tf_op jit(solution)/shard_map/psum | solution.py:39
  354.4 1.4 multiply_add_fusion
  355.9 0.3 copy.27
  356.4 46.9 %custom-call.16 = f32[4,128,128]{2,1,0:T(8,128)S(1)} custom-call(f32[4,128,128]{2,1,0:T(8,128)S(1)} %cholesky.122), custom_call_target="Cholesky" | custom-call | tf_op jit(solution)/shard_map/jit(cholesky)/cholesky | solution.py:40
  403.3 39.3 %custom-call.17 = f32[4,1,128,128]{2,3,1,0:T(8,128)S(1)} custom-call(f32[4,1,128,128]{3,2,1,0:T(8,128)S(1)} %select_bitcast_fusion), custom_call_target="InvertDiagBlocksLowerTriangular" | custom-call | tf_op jit(solution)/shard_map/jit(cholesky)/cholesky | solution.py:40
  442.7 0.4 constant_dynamic-update-slice_fusion.1
  443.1 0.7 convolution_subtract_fusion.1
  443.8 46.9 %custom-call.18 = f32[4,128,128]{2,1,0:T(8,128)S(1)} custom-call(f32[4,128,128]{2,1,0:T(8,128)S(1)} %convolution_subtract_fusion.1), custom_call_target="Cholesky" | custom-call | tf_op jit(solution)/shard_map/jit(cholesky)/cholesky | solution.py:40
  491.0 0.2 select_select_fusion.1
  491.3 5.4 while.1
  491.3 0.6 fusion.25
  491.9 2.1 bitcast_dynamic-update-slice_fusion.2
  494.0 0.6 fusion.25
  494.6 2.1 bitcast_dynamic-update-slice_fusion.2
  496.7 79.4 %custom-call.19 = f32[4,2,128,128]{2,3,1,0:T(8,128)S(1)} custom-call(f32[4,2,128,128]{3,2,1,0:T(8,128)} %bitcast.54), custom_call_target="InvertDiagBlocksLowerTriangular" | custom-call | tf_op jit(solution)/shard_map/triangular_solve | solution.py:41
  576.1 0.6 fusion.18
  576.8 1.8 convolution_subtract_fusion
  578.6 1.1 convolution_convert_fusion
  579.7 1.0 pad_maximum_fusion
  580.8 141.7 %all-gather.2.cloned.1.call-done = bf16[4,8192,256]{1,2,0:T(8,128)(2,1)} async-done(((bf16[4,512,256]{1,2,0:T(8,128)(2,1)}), bf16[4,8192,256]{1,2,0:T(8,128)(2,1)}) %all-gather.2.cloned.1.call-update) | async-done | bytes 16777232 | tf_op jit(solution)/shard_map/all_gather | solution.py:47
  722.5 23.5 %fusion = f32[4,256,1024]{2,1,0:T(8,128)} fusion(bf16[4,8192,256]{1,2,0:T(8,128)(2,1)} %all-gather.2.cloned.1.call-done, bf16[8192,1024]{1,0:T(8,128)(2,1)} %param.8), kind=kOutput, calls=%fused_computation.3 | convolution fusion | flops 17179869184 | bytes 37748736 | tf_op jit(solution)/shard_map/fmk,mq->fkq/dot_general | solution.py:45
  746.0 57.5 %reduce-scatter.5.cloned.1.call-done = f32[4,128,1024]{2,1,0:T(8,128)} async-done(((f32[4,256,1024]{2,1,0:T(8,128)}), f32[4,128,1024]{2,1,0:T(8,128)}) %reduce-scatter.5.cloned.1.call-update) | async-done | bytes 2097168 | tf_op jit(solution)/shard_map/reduce_scatter | solution.py:51
  803.5 2.7 convert_element_type.23
  (44 shorter events, 1.4 us)
Async XLA Ops:
  6.5 58.0 %reduce-scatter.3.cloned.1.call-start = ((), (), s32[]{:S(2)}) async-start(), calls=%async_computation.2 | async-start | bytes 2621440 | tf_op jit(solution)/shard_map/reduce_scatter | solution.py:22
  23.2 0.7 copy-start.5
  23.2 0.7 copy-start.6
  23.2 1.1 copy-start.4
  23.2 331.2 %all-reduce.3.cloned.1.call-start = ((), (), s32[]{:S(2)}) async-start(), calls=%async_computation.3 | async-start | bytes 2097152 | tf_op jit(solution)/shard_map/psum | solution.py:39
  24.3 42.8 %copy-start.2 = (bf16[4,512,128]{2,1,0:T(8,128)(2,1)}, bf16[4,512,128]{2,1,0:T(8,128)(2,1)S(1)}, u32[]{:S(2)}) copy-start(bf16[4,512,128]{2,1,0:T(8,128)(2,1)S(1)} %bitcast_select_fusion) | copy-start | bytes 1572868
  67.1 655.4 %all-gather.2.cloned.1.call-start = ((), (), s32[]{:S(2)}) async-start(), calls=%async_computation.4 | async-start | bytes 17825792 | tf_op jit(solution)/shard_map/all_gather | solution.py:47
  354.4 1.8 copy-start
  491.0 85.1 %copy-start.1 = (bf16[4,128,512]{1,2,0:T(8,128)(2,1)S(1)}, bf16[4,128,512]{1,2,0:T(8,128)(2,1)}, u32[]{:S(2)}) copy-start(bf16[4,128,512]{1,2,0:T(8,128)(2,1)} %reduce-scatter.3.cloned.1.call-done) | copy-start | bytes 1572868
  491.3 85.5 %copy-start.3 = (bf16[4,512,128]{2,1,0:T(8,128)(2,1)S(1)}, bf16[4,512,128]{2,1,0:T(8,128)(2,1)}, u32[]{:S(2)}) copy-start(bf16[4,512,128]{2,1,0:T(8,128)(2,1)} %copy-done.2) | copy-start | bytes 1572868
  580.7 222.8 %reduce-scatter.5.cloned.1.call-start = ((), (), s32[]{:S(2)}) async-start(), calls=%async_computation.5 | async-start | bytes 6291456 | tf_op jit(solution)/shard_map/reduce_scatter | solution.py:51
Sparse Core Ops, SparseCore 0:
  23.3 41.1 reduce-scatter.2
  67.2 287.1 all-reduce.2
  580.9 141.6 all-gather.1
  746.2 57.3 reduce-scatter.4
where the time goes:
time: 813 us
  waiting for transfers between devices  526 us (65%)
  other arithmetic  224 us (28%)
  matrix products  29.6 us (4%)
  local copies, waits for them, and re-layouts  19.5 us (2%)
  between operations  13.4 us (2%)
    psum x1, waiting for transfers between devices, per_device(): gram_total = lax.psum(gram_part, ('aux', 'orb')) + identity_pad  287 us
    all_gather x1, waiting for transfers between devices, per_device(): lax.all_gather(coeffs, 'aux', axis=1, tiled=True)  142 us
    another operation x10, other arithmetic, per_device(): cholesky_low = jnp.linalg.cholesky(gram_total)  133 us
    another operation x5, other arithmetic, per_device(): lax.linalg.triangular_solve(cholesky_low, initial.astype(jnp.float32), le...  80.7 us
    reduce_scatter x1, waiting for transfers between devices, per_device(): lax.psum_scatter(partial_value, 'orb', scatter_dimension=1, tiled=True)  57.5 us
    reduce_scatter x1, waiting for transfers between devices, per_device(): lax.psum_scatter(picked, 'frag', scatter_dimension=0, tiled=True)  40.2 us
    dot_general x1, matrix products, per_device(): jnp.einsum('fmk,mq->fkq', lax.all_gather(coeffs, 'aux', axis=1, tiled=Tru...  23.5 us
  transfers between devices with their start and end apart: 4, of which 4 were waited for; matrix products, arithmetic and copies ran while one was open for 0% of the time, Pallas kernels for 0%

commit v1 on v0

--- a/solution.py
+++ b/solution.py
@@ -2,6 +2,12 @@
 import jax.numpy as jnp
 from jax import lax
 from jax.sharding import PartitionSpec as P
+
+
+def detail_levels_all_on_mesh(xin, link_axis, axis_name):
+    r1 = lax.psum(xin, axis_name=link_axis)
+    kept_arr = lax.psum(r1, axis_name=axis_name)
+    return kept_arr
 
 
 def per_device(density, bath, factor, frag_index, nfrag, nbath):
@@ -36,7 +42,7 @@
     kmax_cols = initial.shape[2]
     identity_pad = jnp.eye(kmax_cols, dtype=jnp.float32)[None] * (1.0 - live_cols)[:, :, None]
     gram_part = jnp.einsum("fmk,fml->fkl", initial, initial, preferred_element_type=jnp.float32)
-    gram_total = lax.psum(gram_part, ("aux", "orb")) + identity_pad
+    gram_total = detail_levels_all_on_mesh(gram_part, "aux", "orb") + identity_pad
     cholesky_low = jnp.linalg.cholesky(gram_total)
     coeffs = lax.linalg.triangular_solve(
         cholesky_low, initial.astype(jnp.float32), left_side=False, lower=True, transpose_a=True

time: 813 us -> 640 us (0.79)
  waiting for transfers between devices: 526 us -> 353 us
    psum x1 -> x2, waiting for transfers between devices: 287 us -> 135 us  [the longest x1 86.2 us: detail_levels_all_on_mesh(): r1 = lax.psum(xin, axis_name=link_axis)]
    all_gather x1, waiting for transfers between devices: 142 us -> 120 us  [per_device(): lax.all_gather(coeffs, 'aux', axis=1, tiled=True)]
  transfers between devices with their start and end apart: 4 -> 5, of which waited for: 4 -> 5; matrix products, arithmetic and copies ran while one was open for 0% -> 0% of each run, Pallas kernels for 0% -> 0%
where the time goes in v1:
time: 640 us
  waiting for transfers between devices  353 us (55%)
  other arithmetic  224 us (35%)
  matrix products  29.6 us (5%)
  local copies, waits for them, and re-layouts  19.5 us (3%)
  between operations  13.4 us (2%)
    another operation x10, other arithmetic, per_device(): cholesky_low = jnp.linalg.cholesky(gram_total)  133 us
    all_gather x1, waiting for transfers between devices, per_device(): lax.all_gather(coeffs, 'aux', axis=1, tiled=True)  120 us
    psum x1, waiting for transfers between devices, detail_levels_all_on_mesh(): r1 = lax.psum(xin, axis_name=link_axis)  86.2 us
    another operation x5, other arithmetic, per_device(): lax.linalg.triangular_solve(cholesky_low, initial.astype(jnp.float32), le...  80.7 us
    reduce_scatter x1, waiting for transfers between devices, per_device(): lax.psum_scatter(partial_value, 'orb', scatter_dimension=1, tiled=True)  57.5 us
    psum x1, waiting for transfers between devices, detail_levels_all_on_mesh(): kept_arr = lax.psum(r1, axis_name=axis_name)  49.2 us
    reduce_scatter x1, waiting for transfers between devices, per_device(): lax.psum_scatter(picked, 'frag', scatter_dimension=0, tiled=True)  40.2 us
    dot_general x1, matrix products, per_device(): jnp.einsum('fmk,mq->fkq', lax.all_gather(coeffs, 'aux', axis=1, tiled=Tru...  23.5 us
  transfers between devices with their start and end apart: 5, of which 5 were waited for; matrix products, arithmetic and copies ran while one was open for 0% of the time, Pallas kernels for 0%

profile of v1, /device:TPU:1, one launch (start us, length us, event | category | flops | bytes accessed | tf_op | source)
XLA Modules:
  0.0 639.5 jit_solution(6426710730251401105)
XLA Ops:
  6.5 0.7 compare_and_fusion
  7.3 10.3 %gather_fusion = bf16[2048,512]{1,0:T(8,128)(2,1)S(1)} fusion(bf16[4096,512]{1,0:T(8,128)(2,1)} %bitcast.50, s32[2048]{0:T(1024)S(1)} %broadcast_clamp_fusion), kind=kCustom, calls=%fused_computation | custom fusion | bytes 4202496 | tf_op jit(solution)/shard_map/jit(_take)/gather | solution.py:24
  17.6 2.4 copy.24
  20.0 3.2 select_select_fusion
  23.3 0.6 copy-done.5
  24.3 40.2 %reduce-scatter.3.cloned.1.call-done = bf16[4,128,512]{1,2,0:T(8,128)(2,1)} async-done(((bf16[16,128,512]{1,2,0:T(8,128)(2,1)}), bf16[4,128,512]{1,2,0:T(8,128)(2,1)}) %reduce-scatter.3.cloned.1.call-update) | async-done | bytes 524304 | tf_op jit(solution)/shard_map/reduce_scatter | solution.py:28
  64.5 1.1 fusion.8
  65.6 1.5 fusion.2
  67.2 86.2 %all-reduce.4.cloned.1.call-done = f32[4,256,256]{1,2,0:T(8,128)} async-done(((f32[4,256,256]{1,2,0:T(8,128)}), f32[4,256,256]{1,2,0:T(8,128)}) %all-reduce.4.cloned.1.call-update) | async-done | bytes 1048592 | tf_op jit(solution)/shard_map/psum | solution.py:8
  153.4 0.2 all-gather.2.cloned.1.call-start
  153.8 49.2 %all-reduce.6.cloned.1.call-done = f32[4,256,256]{1,2,0:T(8,128)} async-done(((f32[4,256,256]{1,2,0:T(8,128)}), f32[4,256,256]{1,2,0:T(8,128)}) %all-reduce.6.cloned.1.call-update) | async-done | bytes 1048592 | tf_op jit(solution)/shard_map/psum | solution.py:9
  203.0 1.4 multiply_add_fusion
  204.5 0.3 copy.27
  205.0 46.9 %custom-call.16 = f32[4,128,128]{2,1,0:T(8,128)S(1)} custom-call(f32[4,128,128]{2,1,0:T(8,128)S(1)} %cholesky.122), custom_call_target="Cholesky" | custom-call | tf_op jit(solution)/shard_map/jit(cholesky)/cholesky | solution.py:46
  251.9 39.3 %custom-call.17 = f32[4,1,128,128]{2,3,1,0:T(8,128)S(1)} custom-call(f32[4,1,128,128]{3,2,1,0:T(8,128)S(1)} %select_bitcast_fusion), custom_call_target="InvertDiagBlocksLowerTriangular" | custom-call | tf_op jit(solution)/shard_map/jit(cholesky)/cholesky | solution.py:46
  291.4 0.4 constant_dynamic-update-slice_fusion.1
  291.8 0.7 convolution_subtract_fusion.1
  292.4 46.9 %custom-call.18 = f32[4,128,128]{2,1,0:T(8,128)S(1)} custom-call(f32[4,128,128]{2,1,0:T(8,128)S(1)} %convolution_subtract_fusion.1), custom_call_target="Cholesky" | custom-call | tf_op jit(solution)/shard_map/jit(cholesky)/cholesky | solution.py:46
  339.9 5.4 while.1
  339.9 0.6 fusion.25
  340.5 2.1 bitcast_dynamic-update-slice_fusion.2
  342.6 0.6 fusion.25
  343.2 2.1 bitcast_dynamic-update-slice_fusion.2
  345.3 79.4 %custom-call.19 = f32[4,2,128,128]{2,3,1,0:T(8,128)S(1)} custom-call(f32[4,2,128,128]{3,2,1,0:T(8,128)} %bitcast.54), custom_call_target="InvertDiagBlocksLowerTriangular" | custom-call | tf_op jit(solution)/shard_map/triangular_solve | solution.py:47
  424.7 0.6 fusion.18
  425.4 1.8 convolution_subtract_fusion
  427.2 1.1 convolution_convert_fusion
  428.3 1.0 pad_maximum_fusion
  429.4 119.8 %all-gather.2.cloned.1.call-done = bf16[4,8192,256]{1,2,0:T(8,128)(2,1)} async-done(((bf16[4,512,256]{1,2,0:T(8,128)(2,1)}), bf16[4,8192,256]{1,2,0:T(8,128)(2,1)}) %all-gather.2.cloned.1.call-update) | async-done | bytes 16777232 | tf_op jit(solution)/shard_map/all_gather | solution.py:53
  549.2 23.5 %fusion = f32[4,256,1024]{2,1,0:T(8,128)} fusion(bf16[4,8192,256]{1,2,0:T(8,128)(2,1)} %all-gather.2.cloned.1.call-done, bf16[8192,1024]{1,0:T(8,128)(2,1)} %param.8), kind=kOutput, calls=%fused_computation.3 | convolution fusion | flops 17179869184 | bytes 37748736 | tf_op jit(solution)/shard_map/fmk,mq->fkq/dot_general | solution.py:51
  572.8 57.5 %reduce-scatter.5.cloned.1.call-done = f32[4,128,1024]{2,1,0:T(8,128)} async-done(((f32[4,256,1024]{2,1,0:T(8,128)}), f32[4,128,1024]{2,1,0:T(8,128)}) %reduce-scatter.5.cloned.1.call-update) | async-done | bytes 2097168 | tf_op jit(solution)/shard_map/reduce_scatter | solution.py:57
  630.3 2.7 convert_element_type.23
  (47 shorter events, 1.6 us)
Async XLA Ops:
  6.5 58.0 %reduce-scatter.3.cloned.1.call-start = ((), (), s32[]{:S(2)}) async-start(), calls=%async_computation.2 | async-start | bytes 2621440 | tf_op jit(solution)/shard_map/reduce_scatter | solution.py:28
  23.2 0.7 copy-start.5
  23.2 0.7 copy-start.6
  23.2 1.1 copy-start.4
  23.2 130.2 %all-reduce.4.cloned.1.call-start = ((), (), s32[]{:S(2)}) async-start(), calls=%async_computation.3 | async-start | bytes 2097152 | tf_op jit(solution)/shard_map/psum | solution.py:8
  24.3 42.8 %copy-start.2 = (bf16[4,512,128]{2,1,0:T(8,128)(2,1)}, bf16[4,512,128]{2,1,0:T(8,128)(2,1)S(1)}, u32[]{:S(2)}) copy-start(bf16[4,512,128]{2,1,0:T(8,128)(2,1)S(1)} %bitcast_select_fusion) | copy-start | bytes 1572868
  67.1 135.9 %all-reduce.6.cloned.1.call-start = ((), (), s32[]{:S(2)}) async-start(), calls=%async_computation.4 | async-start | bytes 2097152 | tf_op jit(solution)/shard_map/psum | solution.py:9
  153.4 395.8 %all-gather.2.cloned.1.call-start = ((), (), s32[]{:S(2)}) async-start(), calls=%async_computation.5 | async-start | bytes 17825792 | tf_op jit(solution)/shard_map/all_gather | solution.py:53
  203.0 1.8 copy-start
  339.6 85.1 %copy-start.1 = (bf16[4,128,512]{1,2,0:T(8,128)(2,1)S(1)}, bf16[4,128,512]{1,2,0:T(8,128)(2,1)}, u32[]{:S(2)}) copy-start(bf16[4,128,512]{1,2,0:T(8,128)(2,1)} %reduce-scatter.3.cloned.1.call-done) | copy-start | bytes 1572868
  339.9 85.5 %copy-start.3 = (bf16[4,512,128]{2,1,0:T(8,128)(2,1)S(1)}, bf16[4,512,128]{2,1,0:T(8,128)(2,1)}, u32[]{:S(2)}) copy-start(bf16[4,512,128]{2,1,0:T(8,128)(2,1)} %copy-done.2) | copy-start | bytes 1572868
  429.4 200.9 %reduce-scatter.5.cloned.1.call-start = ((), (), s32[]{:S(2)}) async-start(), calls=%async_computation.6 | async-start | bytes 6291456 | tf_op jit(solution)/shard_map/reduce_scatter | solution.py:57
Sparse Core Ops, SparseCore 0:
  23.3 41.1 reduce-scatter.2
  67.8 85.5 all-reduce.3
  155.9 47.1 all-reduce.5
  429.5 119.7 all-gather.1
  572.9 57.3 reduce-scatter.4
